TPU v7x, 512 devices: a whole 4x8x8 slice. The times are simulated.
512 devices in a mesh: gs: 128 (over y, z, core), view: 4 (over x).
Axes of the slice: x: 4, y: 8, z: 8, core: 2. Of those that a mesh axis runs over, the one named last changes fastest.
Arguments:
- features: bfloat16 [131072, 128], P('gs'), may hold values from -6 to 6
- geometry: float32 [4, 9, 131072], P('view', None, 'gs'), as said below
- decoder: bfloat16 [128, 512], replicated, may hold values from -0.5 to 0.5
- teacher: bfloat16 [4, 131072, 512], P('view', 'gs'), may hold values from -3 to 3
- images: float32 [4, 3, 131072], P('view', None, 'gs'), may hold values from 0 to 1
- send_index: int32 [4, 128, 1024], P('view', 'gs'), may hold values from 0 to 1023, as said below
- tile_lists: int32 [4, 512, 8], P('view', 'gs'), may hold values from 0 to 7, as said below
- tile_lengths: int32 [4, 512], P('view', 'gs'), may hold values from 2 to 8
Outputs:
- feature_grad: float32 [131072, 128], P(('gs', 'view'))
- geometry_grad: float32 [4, 9, 131072], P('view', None, 'gs')
- decoder_grad: float32 [128, 512], replicated
Inputs may be any that keep to these rules, and one draw needn't show every extreme that they name: `send_index`: each row (one view, one source device) is a permutation of 0 .. 1023; positions k * 8 to (k + 1) * 8 - 1 hold the Gaussians sent to the device of gs index k. `tile_lists`: the 8 entries of a row are distinct. `geometry`: opacity logits lie in -7.5 .. -4, log conics between -2 log 16 and -2 log 16 + 2 log 4, shears in -2 .. 2, colors in 0 .. 1.
All inputs are finite; a program needn't handle non-finite values.
Results may differ from a plain program's by a relative error of at most 0.0017.
Values may be sent and summed in bfloat16 or wider, within the bound.
A program may use at most 64 MiB of HBM per device.

v0:
```python
import math
import jax
import jax.numpy as jnp
from jax import lax
from jax.sharding import PartitionSpec as P

FEAT = 128
CT = 512
TS = 16
BLK = 128
LIST = 8


def composite(tile_geo, alive_mask, pixel_x, pixel_y):
    delta_x = pixel_x[:, None] - tile_geo[0][None, :]
    delta_y = pixel_y[:, None] - tile_geo[1][None, :]
    conic_a = jnp.exp(tile_geo[2])
    conic_c = jnp.exp(tile_geo[3])
    conic_b = 0.8 * jnp.tanh(tile_geo[4]) * jnp.exp(0.5 * (tile_geo[2] + tile_geo[3]))
    exponent = -0.5 * (
        conic_a * delta_x * delta_x
        + 2.0 * conic_b * delta_x * delta_y
        + conic_c * delta_y * delta_y
    )
    opacity = alive_mask * jax.nn.sigmoid(tile_geo[5])
    alpha_val = opacity[None, :] * jnp.exp(exponent)
    log_keep = jnp.log1p(-alpha_val)
    pixel_count = pixel_x.shape[0]
    blocked = log_keep.reshape(pixel_count, LIST, BLK)
    inner = jnp.cumsum(blocked, axis=2) - blocked
    block_sums = jnp.sum(blocked, axis=2)
    outer = jnp.cumsum(block_sums, axis=1) - block_sums
    before = (inner + outer[:, :, None]).reshape(pixel_count, LIST * BLK)
    weights = alpha_val * jnp.exp(before)
    pixel_color = jnp.einsum("pi,ci->cp", weights, tile_geo[6:9], precision=lax.Precision.HIGHEST)
    return (weights, pixel_color)


def device_terms(
    recv_geo, recv_feat, decoder, teacher_dev, images_dev, lists, lengths, shard_index
):
    nblocks = recv_feat.shape[0] // BLK
    tile_pixels = TS * TS
    geo_blocks = recv_geo.reshape(9, nblocks, BLK)
    feat_blocks = recv_feat.reshape(nblocks, BLK, FEAT)
    within = jnp.arange(tile_pixels, dtype=jnp.int32)
    block_range = jnp.arange(nblocks, dtype=jnp.int32)
    slot_range = jnp.arange(LIST, dtype=jnp.int32)

    def tile_step(totals, tile_index):
        decoder_sum, geo_acc, feat_acc = totals
        block_ids = lists[tile_index]
        count = lengths[tile_index]
        alive_mask = jnp.broadcast_to(
            (slot_range < count).astype(jnp.float32)[:, None], (LIST, BLK)
        ).reshape(LIST * BLK)
        tile_geo = jnp.take(geo_blocks, block_ids, axis=1).reshape(9, LIST * BLK)
        feat_tile = jnp.take(feat_blocks, block_ids, axis=0).reshape(LIST * BLK, FEAT)
        column = 2 * TS * (shard_index % 30) + TS * (tile_index % 2) + within % TS
        row_index = 2 * TS * (shard_index // 30) + TS * (tile_index // 2) + within // TS
        pixel_x = column.astype(jnp.float32) + 0.5
        pixel_y = row_index.astype(jnp.float32) + 0.5
        (weights, pixel_color), pullback = jax.vjp(
            lambda geo_part: composite(geo_part, alive_mask, pixel_x, pixel_y), tile_geo
        )
        weight_b = weights.astype(jnp.bfloat16)
        rendered = jnp.dot(weight_b, feat_tile, preferred_element_type=jnp.float32).astype(
            jnp.bfloat16
        )
        pred = jnp.dot(rendered, decoder, preferred_element_type=jnp.float32)
        teacher_rows = lax.dynamic_slice_in_dim(
            teacher_dev, tile_index * tile_pixels, tile_pixels, 0
        )
        error_feat = pred - teacher_rows.astype(jnp.float32)
        gpred = (error_feat / jnp.sqrt(error_feat * error_feat + 0.04)).astype(jnp.bfloat16)
        grender = lax.dot_general(
            gpred, decoder, (((1,), (1,)), ((), ())), preferred_element_type=jnp.float32
        ).astype(jnp.bfloat16)
        decoder_sum = decoder_sum + lax.dot_general(
            rendered, gpred, (((0,), (0,)), ((), ())), preferred_element_type=jnp.float32
        )
        image_cols = lax.dynamic_slice_in_dim(images_dev, tile_index * tile_pixels, tile_pixels, 1)
        error_color = pixel_color - image_cols
        gcolor = error_color / jnp.sqrt(error_color * error_color + 0.04)
        gweight = lax.dot_general(
            grender, feat_tile, (((1,), (1,)), ((), ())), preferred_element_type=jnp.float32
        )
        gfeat_tile = lax.dot_general(
            weight_b, grender, (((0,), (0,)), ((), ())), preferred_element_type=jnp.float32
        )
        (ggeo_tile,) = pullback((gweight, gcolor))
        hits = (block_ids[:, None] == block_range[None, :]).astype(jnp.float32)
        geo_acc = geo_acc + jnp.einsum(
            "clb,ln->cnb", ggeo_tile.reshape(9, LIST, BLK), hits, precision=lax.Precision.HIGHEST
        )
        feat_acc = feat_acc + jnp.einsum(
            "ln,lbf->nbf",
            hits,
            gfeat_tile.reshape(LIST, BLK, FEAT),
            precision=lax.Precision.HIGHEST,
        )
        return ((decoder_sum, geo_acc, feat_acc), None)

    start_totals = (
        jnp.zeros((FEAT, CT), jnp.float32),
        jnp.zeros((9, nblocks, BLK), jnp.float32),
        jnp.zeros((nblocks, BLK, FEAT), jnp.float32),
    )
    tile_range = jnp.arange(lists.shape[0], dtype=jnp.int32)
    (decoder_sum, geo_acc, feat_acc), _ = lax.scan(tile_step, start_totals, tile_range)
    return (decoder_sum, geo_acc.reshape(9, nblocks * BLK), feat_acc.reshape(nblocks * BLK, FEAT))


def on_device(features, geometry, decoder, teacher, images, send_index, tile_lists, tile_lengths):
    send_order = send_index[0, 0]
    shard_index = lax.axis_index("gs")
    geo_send = jnp.take(geometry[0], send_order, axis=1)
    recv_geo = lax.all_to_all(geo_send, "gs", split_axis=1, concat_axis=1, tiled=True)
    feat_send = jnp.take(features, send_order, axis=0)
    recv_feat = lax.all_to_all(feat_send, "gs", split_axis=0, concat_axis=0, tiled=True)
    decoder_sum, geo_acc, feat_acc = device_terms(
        recv_geo,
        recv_feat,
        decoder,
        teacher[0],
        images[0],
        tile_lists[0],
        tile_lengths[0],
        shard_index,
    )
    returned_geo = lax.all_to_all(geo_acc, "gs", split_axis=1, concat_axis=1, tiled=True)
    returned_feat = lax.all_to_all(feat_acc, "gs", split_axis=0, concat_axis=0, tiled=True)
    geo_own = jnp.zeros_like(returned_geo).at[:, send_order].set(returned_geo)
    feat_own = jnp.zeros_like(returned_feat).at[send_order].set(returned_feat)
    quarter = feat_own.shape[0] // lax.axis_size("view")
    summed = lax.psum(feat_own, "view")
    feature_grad = lax.dynamic_slice_in_dim(summed, lax.axis_index("view") * quarter, quarter, 0)
    pixel_total = lax.axis_size("gs") * lax.axis_size("view") * tile_lists.shape[1] * TS * TS
    decoder_grad = lax.psum(decoder_sum, ("gs", "view")) * (1.0 / math.sqrt(pixel_total))
    return (feature_grad, geo_own[None], decoder_grad)


def solution(mesh):
    placed = (
        P("gs", None),
        P("view", None, "gs"),
        P(),
        P("view", "gs", None),
        P("view", None, "gs"),
        P("view", "gs", None),
        P("view", "gs", None),
        P("view", "gs"),
    )
    return jax.shard_map(
        on_device,
        mesh=mesh,
        in_specs=placed,
        out_specs=(P(("gs", "view"), None), P("view", None, "gs"), P()),
        check_vma=False,
    )
```

profile of v0, /device:TPU:8, one launch (start us, length us, event | category | flops | bytes accessed | tf_op | source)
XLA Modules:
  0.0 610.4 jit_solution(10011325874883574381)
XLA Ops:
  10.2 2.8 gather_fusion.2
  14.1 17.4 %all-to-all-start = ((f32[9,128,8]{0,2,1:T(8,128)}), f32[9,128,8]{0,2,1:T(8,128)S(1)}, u32[]{:S(2)}, u32[]{:S(2)}) async-start(f32[9,128,8]{0,2,1:T(8,128)} %bitcast_select_fusion.1), calls=%async_computation | async-start | bytes 1048576 | tf_op jit(solution)/shard_map/all_to_all | solution.py:118
  31.5 3.2 gather_fusion.3
  35.6 16.2 %all-to-all-done = f32[9,128,8]{0,2,1:T(8,128)S(1)} async-done(((f32[9,128,8]{0,2,1:T(8,128)}), f32[9,128,8]{0,2,1:T(8,128)S(1)}, u32[]{:S(2)}, u32[]{:S(2)}) %all-to-all-start) | async-done | bytes 36896 | tf_op jit(solution)/shard_map/all_to_all | solution.py:118
  51.8 6.5 %all-to-all-start.1 = ((bf16[128,8,128]{2,1,0:T(8,128)(2,1)}), bf16[128,8,128]{2,1,0:T(8,128)(2,1)S(1)}, u32[]{:S(2)}, u32[]{:S(2)}) async-start(bf16[128,8,128]{2,1,0:T(8,128)(2,1)} %bitcast_select_fusion.2), calls=%async_computation.1 | async-start | bytes 524288 | tf_op jit(solution)/shard_map/all_to_all | solution.py:120
  60.4 12.6 %all-to-all-done.1 = bf16[128,8,128]{2,1,0:T(8,128)(2,1)S(1)} async-done(((bf16[128,8,128]{2,1,0:T(8,128)(2,1)}), bf16[128,8,128]{2,1,0:T(8,128)(2,1)S(1)}, u32[]{:S(2)}, u32[]{:S(2)}) %all-to-all-start.1) | async-done | bytes 262176 | tf_op jit(solution)/shard_map/all_to_all | solution.py:120
  73.7 187.1 %while.21 = (s32[]{:T(128)}, f32[128,512]{1,0:T(8,128)}, f32[9,8,128]{2,1,0:T(8,128)}, f32[8,128,128]{2,0,1:T(8,128)}, s32[4]{0:T(128)S(1)}, /*index=5*/s32[4]{0...) while((s32[]{:T(128)}, f32[128,512]{1,0:T(8,128)}, ...), condition=%wide.region_13.14_spmd.clone.clone, body=%wide.region_0.13_spmd.clone.clone.sunk | while | flops 448201472 | bytes 62394652 | solution.py:110
  89.3 2.2 exponential_multiply_fusion.2
  107.0 3.4 fusion.167
  114.7 2.3 fusion.168
  135.2 2.2 exponential_multiply_fusion.2
  147.6 2.3 convolution_add_fusion.8
  154.0 3.4 fusion.167
  161.7 2.3 fusion.168
  182.3 2.2 exponential_multiply_fusion.2
  194.7 2.3 convolution_add_fusion.8
  201.1 3.4 fusion.167
  208.8 2.3 fusion.168
  229.3 2.2 exponential_multiply_fusion.2
  237.1 1.8 fusion.171
  241.7 2.3 convolution_add_fusion.8
  248.1 3.4 fusion.167
  255.8 2.3 fusion.168
  260.8 1.9 copy.80
  262.7 6.5 %all-to-all-start.2 = ((f32[128,8,128]{2,1,0:T(8,128)}), f32[128,8,128]{2,1,0:T(8,128)S(1)}, u32[]{:S(2)}, u32[]{:S(2)}) async-start(f32[128,8,128]{2,1,0:T(8,128)} %bitcast.11), calls=%async_computation.2 | async-start | bytes 1048576 | tf_op jit(solution)/shard_map/all_to_all | solution.py:132
  270.0 19.5 %all-to-all-done.2 = f32[128,8,128]{2,1,0:T(8,128)S(1)} async-done(((f32[128,8,128]{2,1,0:T(8,128)}), f32[128,8,128]{2,1,0:T(8,128)S(1)}, u32[]{:S(2)}, u32[]{:S(2)}) %all-to-all-start.2) | async-done | bytes 524320 | tf_op jit(solution)/shard_map/all_to_all | solution.py:132
  289.5 4.0 scatter_custom_fusion
  295.4 6.4 %all-to-all-start.3 = ((f32[9,128,8]{0,2,1:T(8,128)}), f32[9,128,8]{0,2,1:T(8,128)S(1)}, u32[]{:S(2)}, u32[]{:S(2)}) async-start(f32[9,128,8]{0,2,1:T(8,128)} %bitcast.13), calls=%async_computation.3 | async-start | bytes 1048576 | tf_op jit(solution)/shard_map/all_to_all | solution.py:131
  301.7 20.4 %all-to-all-done.3 = f32[9,128,8]{0,2,1:T(8,128)S(1)} async-done(((f32[9,128,8]{0,2,1:T(8,128)}), f32[9,128,8]{0,2,1:T(8,128)S(1)}, u32[]{:S(2)}, u32[]{:S(2)}) %all-to-all-start.3) | async-done | bytes 36896 | tf_op jit(solution)/shard_map/all_to_all | solution.py:131
  322.2 3.4 scatter_custom_fusion.1
  326.4 222.5 %all-reduce.14.cloned.1.call-done = f32[128,512]{1,0:T(8,128)} async-done(((f32[128,512]{1,0:T(8,128)}), f32[128,512]{1,0:T(8,128)}) %all-reduce.14.cloned.1.call-update) | async-done | bytes 262160 | tf_op jit(solution)/shard_map/psum | solution.py:139
  550.5 51.4 %all-reduce.12.cloned.1.call-done = f32[1024,128]{1,0:T(8,128)} async-done(((f32[1024,128]{1,0:T(8,128)}), f32[1024,128]{1,0:T(8,128)}) %all-reduce.12.cloned.1.call-update) | async-done | bytes 524304 | tf_op jit(solution)/shard_map/psum | solution.py:136
  (517 shorter events, 140.9 us)
Async XLA Ops:
  7.2 24.3 %copy-start = (bf16[1024,128]{1,0:T(8,128)(2,1)S(1)}, bf16[1024,128]{1,0:T(8,128)(2,1)}, u32[]{:S(2)}) copy-start(bf16[1024,128]{1,0:T(8,128)(2,1)} %param.10) | copy-start | bytes 786436
  14.1 37.7 %all-to-all-start = ((f32[9,128,8]{0,2,1:T(8,128)}), f32[9,128,8]{0,2,1:T(8,128)S(1)}, u32[]{:S(2)}, u32[]{:S(2)}) async-start(f32[9,128,8]{0,2,1:T(8,128)} %bitcast_select_fusion.1), calls=%async_computation | async-start | bytes 1048576 | tf_op jit(solution)/shard_map/all_to_all | solution.py:118
  51.8 21.3 %all-to-all-start.1 = ((bf16[128,8,128]{2,1,0:T(8,128)(2,1)}), bf16[128,8,128]{2,1,0:T(8,128)(2,1)S(1)}, u32[]{:S(2)}, u32[]{:S(2)}) async-start(bf16[128,8,128]{2,1,0:T(8,128)(2,1)} %bitcast_select_fusion.2), calls=%async_computation.1 | async-start | bytes 524288 | tf_op jit(solution)/shard_map/all_to_all | solution.py:120
  73.7 13.7 %copy-start.8 = (bf16[8,128,128]{2,1,0:T(8,128)(2,1)}, bf16[8,128,128]{2,1,0:T(8,128)(2,1)S(1)}, u32[]{:S(2)}) copy-start(bf16[8,128,128]{2,1,0:T(8,128)(2,1)S(1)} %get-tuple-element.843) | copy-start | bytes 786436 | tf_op jit(solution)/shard_map/while
  81.3 22.9 %copy-start.21 = (f32[256]{0:T(256)}, f32[256]{0:T(256)S(1)}, u32[]{:S(2)}) copy-start(f32[256]{0:T(256)S(1)} %get-tuple-element.768) | copy-start | bytes 3076 | tf_op jit(solution)/shard_map/while
  81.3 22.9 %copy-start.23 = (f32[256]{0:T(256)}, f32[256]{0:T(256)S(1)}, u32[]{:S(2)}) copy-start(f32[256]{0:T(256)S(1)} %get-tuple-element.765) | copy-start | bytes 3076 | tf_op jit(solution)/shard_map/while
  82.0 19.6 %copy-start.28 = (s32[8]{0:T(128)}, s32[8]{0:T(128)S(1)}, u32[]{:S(2)}) copy-start(s32[8]{0:T(128)S(1)} %get-tuple-element.785) | copy-start | bytes 100 | tf_op jit(solution)/shard_map/while
  84.2 18.9 %copy-start.5 = (f32[9,8,128]{2,0,1:T(8,128)}, f32[9,8,128]{2,0,1:T(8,128)S(1)}, u32[]{:S(2)}) copy-start(f32[9,8,128]{2,0,1:T(8,128)S(1)} %select_bitcast_fusion.2) | copy-start | bytes 110596 | tf_op jit(solution)/shard_map/while
  84.9 19.4 %copy-start.11 = (f32[1,8,128]{2,0,1:T(1,128)}, f32[1,8,128]{2,0,1:T(1,128)S(1)}, u32[]{:S(2)}) copy-start(f32[1,8,128]{2,0,1:T(1,128)S(1)} %get-tuple-element.769) | copy-start | bytes 12292 | tf_op jit(solution)/shard_map/while
  85.5 18.8 %copy-start.16 = (f32[1024]{0:T(1024)}, f32[1024]{0:T(1024)S(1)}, u32[]{:S(2)}) copy-start(f32[1024]{0:T(1024)S(1)} %bitcast_multiply_fusion.8) | copy-start | bytes 12292 | tf_op jit(solution)/shard_map/while
  127.3 24.0 %copy-start.21 = (f32[256]{0:T(256)}, f32[256]{0:T(256)S(1)}, u32[]{:S(2)}) copy-start(f32[256]{0:T(256)S(1)} %get-tuple-element.768) | copy-start | bytes 3076 | tf_op jit(solution)/shard_map/while
  127.3 24.0 %copy-start.23 = (f32[256]{0:T(256)}, f32[256]{0:T(256)S(1)}, u32[]{:S(2)}) copy-start(f32[256]{0:T(256)S(1)} %get-tuple-element.765) | copy-start | bytes 3076 | tf_op jit(solution)/shard_map/while
  128.0 19.6 %copy-start.28 = (s32[8]{0:T(128)}, s32[8]{0:T(128)S(1)}, u32[]{:S(2)}) copy-start(s32[8]{0:T(128)S(1)} %get-tuple-element.785) | copy-start | bytes 100 | tf_op jit(solution)/shard_map/while
  130.2 20.0 %copy-start.5 = (f32[9,8,128]{2,0,1:T(8,128)}, f32[9,8,128]{2,0,1:T(8,128)S(1)}, u32[]{:S(2)}) copy-start(f32[9,8,128]{2,0,1:T(8,128)S(1)} %select_bitcast_fusion.2) | copy-start | bytes 110596 | tf_op jit(solution)/shard_map/while
  130.8 20.5 %copy-start.11 = (f32[1,8,128]{2,0,1:T(1,128)}, f32[1,8,128]{2,0,1:T(1,128)S(1)}, u32[]{:S(2)}) copy-start(f32[1,8,128]{2,0,1:T(1,128)S(1)} %get-tuple-element.769) | copy-start | bytes 12292 | tf_op jit(solution)/shard_map/while
  131.4 19.9 %copy-start.16 = (f32[1024]{0:T(1024)}, f32[1024]{0:T(1024)S(1)}, u32[]{:S(2)}) copy-start(f32[1024]{0:T(1024)S(1)} %bitcast_multiply_fusion.8) | copy-start | bytes 12292 | tf_op jit(solution)/shard_map/while
  174.3 24.0 %copy-start.21 = (f32[256]{0:T(256)}, f32[256]{0:T(256)S(1)}, u32[]{:S(2)}) copy-start(f32[256]{0:T(256)S(1)} %get-tuple-element.768) | copy-start | bytes 3076 | tf_op jit(solution)/shard_map/while
  174.3 24.0 %copy-start.23 = (f32[256]{0:T(256)}, f32[256]{0:T(256)S(1)}, u32[]{:S(2)}) copy-start(f32[256]{0:T(256)S(1)} %get-tuple-element.765) | copy-start | bytes 3076 | tf_op jit(solution)/shard_map/while
  175.0 19.6 %copy-start.28 = (s32[8]{0:T(128)}, s32[8]{0:T(128)S(1)}, u32[]{:S(2)}) copy-start(s32[8]{0:T(128)S(1)} %get-tuple-element.785) | copy-start | bytes 100 | tf_op jit(solution)/shard_map/while
  177.2 20.0 %copy-start.5 = (f32[9,8,128]{2,0,1:T(8,128)}, f32[9,8,128]{2,0,1:T(8,128)S(1)}, u32[]{:S(2)}) copy-start(f32[9,8,128]{2,0,1:T(8,128)S(1)} %select_bitcast_fusion.2) | copy-start | bytes 110596 | tf_op jit(solution)/shard_map/while
  177.8 20.5 %copy-start.11 = (f32[1,8,128]{2,0,1:T(1,128)}, f32[1,8,128]{2,0,1:T(1,128)S(1)}, u32[]{:S(2)}) copy-start(f32[1,8,128]{2,0,1:T(1,128)S(1)} %get-tuple-element.769) | copy-start | bytes 12292 | tf_op jit(solution)/shard_map/while
  178.4 19.9 %copy-start.16 = (f32[1024]{0:T(1024)}, f32[1024]{0:T(1024)S(1)}, u32[]{:S(2)}) copy-start(f32[1024]{0:T(1024)S(1)} %bitcast_multiply_fusion.8) | copy-start | bytes 12292 | tf_op jit(solution)/shard_map/while
  221.3 24.0 %copy-start.21 = (f32[256]{0:T(256)}, f32[256]{0:T(256)S(1)}, u32[]{:S(2)}) copy-start(f32[256]{0:T(256)S(1)} %get-tuple-element.768) | copy-start | bytes 3076 | tf_op jit(solution)/shard_map/while
  221.3 24.0 %copy-start.23 = (f32[256]{0:T(256)}, f32[256]{0:T(256)S(1)}, u32[]{:S(2)}) copy-start(f32[256]{0:T(256)S(1)} %get-tuple-element.765) | copy-start | bytes 3076 | tf_op jit(solution)/shard_map/while
  222.0 19.6 %copy-start.28 = (s32[8]{0:T(128)}, s32[8]{0:T(128)S(1)}, u32[]{:S(2)}) copy-start(s32[8]{0:T(128)S(1)} %get-tuple-element.785) | copy-start | bytes 100 | tf_op jit(solution)/shard_map/while
  224.2 20.0 %copy-start.5 = (f32[9,8,128]{2,0,1:T(8,128)}, f32[9,8,128]{2,0,1:T(8,128)S(1)}, u32[]{:S(2)}) copy-start(f32[9,8,128]{2,0,1:T(8,128)S(1)} %select_bitcast_fusion.2) | copy-start | bytes 110596 | tf_op jit(solution)/shard_map/while
  224.9 20.5 %copy-start.11 = (f32[1,8,128]{2,0,1:T(1,128)}, f32[1,8,128]{2,0,1:T(1,128)S(1)}, u32[]{:S(2)}) copy-start(f32[1,8,128]{2,0,1:T(1,128)S(1)} %get-tuple-element.769) | copy-start | bytes 12292 | tf_op jit(solution)/shard_map/while
  225.5 19.9 %copy-start.16 = (f32[1024]{0:T(1024)}, f32[1024]{0:T(1024)S(1)}, u32[]{:S(2)}) copy-start(f32[1024]{0:T(1024)S(1)} %bitcast_multiply_fusion.8) | copy-start | bytes 12292 | tf_op jit(solution)/shard_map/while
  262.7 26.8 %all-to-all-start.2 = ((f32[128,8,128]{2,1,0:T(8,128)}), f32[128,8,128]{2,1,0:T(8,128)S(1)}, u32[]{:S(2)}, u32[]{:S(2)}) async-start(f32[128,8,128]{2,1,0:T(8,128)} %bitcast.11), calls=%async_computation.2 | async-start | bytes 1048576 | tf_op jit(solution)/shard_map/all_to_all | solution.py:132
  269.2 279.6 %all-reduce.14.cloned.1.call-start = ((), (), s32[]{:S(2)}) async-start(), calls=%async_computation.5 | async-start | bytes 524288 | tf_op jit(solution)/shard_map/psum | solution.py:139
  269.9 332.0 %all-reduce.12.cloned.1.call-start = ((), (), s32[]{:S(2)}) async-start(), calls=%async_computation.4 | async-start | bytes 1048576 | tf_op jit(solution)/shard_map/psum | solution.py:136
  295.4 26.8 %all-to-all-start.3 = ((f32[9,128,8]{0,2,1:T(8,128)}), f32[9,128,8]{0,2,1:T(8,128)S(1)}, u32[]{:S(2)}, u32[]{:S(2)}) async-start(f32[9,128,8]{0,2,1:T(8,128)} %bitcast.13), calls=%async_computation.3 | async-start | bytes 1048576 | tf_op jit(solution)/shard_map/all_to_all | solution.py:131
  (105 other events, 181.8 us)
Sparse Core Ops, SparseCore 0:
  275.6 273.1 all-reduce.13
  551.3 50.6 all-reduce.11
where the time goes:
time: 613 us; the launch traced here: 610 us
  waiting for transfers between devices  343 us (56%)
  local copies, waits for them, and re-layouts  79.9 us (13%)
  other arithmetic  76.6 us (12%)
  matrix products  39.1 us (6%)
  starting transfers between devices  36.8 us (6%)
  loops' own time  20.3 us (3%)
  between operations  14.3 us (2%)
    psum x1, waiting for transfers between devices, on_device(): lax.psum(decoder_sum, ('gs', 'view')) * (1.0 / math.sqrt(pixel_total))  222 us
    psum x1, waiting for transfers between devices, on_device(): summed = lax.psum(feat_own, 'view')  51.4 us
    another operation x8, other arithmetic, composite(): inner = jnp.cumsum(blocked, axis=2) - blocked  22.4 us
    all_to_all x1, waiting for transfers between devices, on_device(): lax.all_to_all(geo_acc, 'gs', split_axis=1, concat_axis=1, tiled=True)  20.4 us
    another operation x1, loops' own time, device_terms(): lax.scan(tile_step, start_totals, tile_range)  20.3 us
    all_to_all x1, waiting for transfers between devices, on_device(): lax.all_to_all(feat_acc, 'gs', split_axis=0, concat_axis=0, tiled=True)  19.5 us
    while x264, local copies, waits for them, and re-layouts  19.3 us
    all_to_all x1, starting transfers between devices, on_device(): lax.all_to_all(geo_send, 'gs', split_axis=1, concat_axis=1, tiled=True)  17.4 us
  transfers between devices with their start and end apart: 6, of which 6 were waited for; matrix products, arithmetic and copies ran while one was open for 3% of the time, Pallas kernels for 0%

commit v1 on v0

--- a/solution.py
+++ b/solution.py
@@ -136,7 +136,8 @@
     summed = lax.psum(feat_own, "view")
     feature_grad = lax.dynamic_slice_in_dim(summed, lax.axis_index("view") * quarter, quarter, 0)
     pixel_total = lax.axis_size("gs") * lax.axis_size("view") * tile_lists.shape[1] * TS * TS
-    decoder_grad = lax.psum(decoder_sum, ("gs", "view")) * (1.0 / math.sqrt(pixel_total))
+    frames_name = lambda view: lax.psum(lax.psum(view, axis_name="view"), axis_name="gs")
+    decoder_grad = frames_name(decoder_sum) * (1.0 / math.sqrt(pixel_total))
     return (feature_grad, geo_own[None], decoder_grad)
 
 

time: 613 us -> 546 us (0.89)
  the two profiles are of different devices: /device:TPU:8 before, /device:TPU:24 now
where the time goes in v1:
time: 546 us; the launch traced here: 543 us
  waiting for transfers between devices  254 us (47%)
  local copies, waits for them, and re-layouts  79.1 us (14%)
  other arithmetic  76.6 us (14%)
  matrix products  39.1 us (7%)
  starting transfers between devices  34 us (6%)
  blocking collectives  26 us (5%)
  loops' own time  20.3 us (4%)
  between operations  14.3 us (3%)
    psum x1, waiting for transfers between devices, on_device(): lax.psum(lax.psum(view, axis_name='view'), axis_name='gs')  189 us
    psum x1, waiting for transfers between devices, on_device(): summed = lax.psum(feat_own, 'view')  39.8 us
    all_to_all x1, blocking collectives, on_device(): lax.all_to_all(feat_acc, 'gs', split_axis=0, concat_axis=0, tiled=True)  26 us
    another operation x8, other arithmetic, composite(): inner = jnp.cumsum(blocked, axis=2) - blocked  22.4 us
    another operation x1, loops' own time, device_terms(): lax.scan(tile_step, start_totals, tile_range)  20.3 us
    while x264, local copies, waits for them, and re-layouts  19.2 us
    all_to_all x1, starting transfers between devices, on_device(): lax.all_to_all(geo_send, 'gs', split_axis=1, concat_axis=1, tiled=True)  17.3 us
    dot_general x12, matrix products, composite(): jnp.einsum('pi,ci->cp', weights, tile_geo[6:9], precision=lax.Precision.H...  17.3 us
  transfers between devices with their start and end apart: 5, of which 4 were waited for; matrix products, arithmetic and copies ran while one was open for 2% of the time, Pallas kernels for 0%

profile of v1, /device:TPU:24, one launch (start us, length us, event | category | flops | bytes accessed | tf_op | source)
XLA Modules:
  0.0 543.4 jit_solution(13660900999529790537)
XLA Ops:
  10.2 2.8 gather_fusion.2
  14.1 17.3 %all-to-all-start = ((f32[9,128,8]{0,2,1:T(8,128)}), f32[9,128,8]{0,2,1:T(8,128)S(1)}, u32[]{:S(2)}, u32[]{:S(2)}) async-start(f32[9,128,8]{0,2,1:T(8,128)} %bitcast_select_fusion.1), calls=%async_computation | async-start | bytes 1048576 | tf_op jit(solution)/shard_map/all_to_all | solution.py:118
  31.4 3.2 gather_fusion.3
  35.6 14.3 %all-to-all-done = f32[9,128,8]{0,2,1:T(8,128)S(1)} async-done(((f32[9,128,8]{0,2,1:T(8,128)}), f32[9,128,8]{0,2,1:T(8,128)S(1)}, u32[]{:S(2)}, u32[]{:S(2)}) %all-to-all-start) | async-done | bytes 36896 | tf_op jit(solution)/shard_map/all_to_all | solution.py:118
  49.9 8.3 %all-to-all-start.1 = ((bf16[128,8,128]{2,1,0:T(8,128)(2,1)}), bf16[128,8,128]{2,1,0:T(8,128)(2,1)S(1)}, u32[]{:S(2)}, u32[]{:S(2)}) async-start(bf16[128,8,128]{2,1,0:T(8,128)(2,1)} %bitcast_select_fusion.2), calls=%async_computation.1 | async-start | bytes 524288 | tf_op jit(solution)/shard_map/all_to_all | solution.py:120
  60.4 10.9 %all-to-all-done.1 = bf16[128,8,128]{2,1,0:T(8,128)(2,1)S(1)} async-done(((bf16[128,8,128]{2,1,0:T(8,128)(2,1)}), bf16[128,8,128]{2,1,0:T(8,128)(2,1)S(1)}, u32[]{:S(2)}, u32[]{:S(2)}) %all-to-all-start.1) | async-done | bytes 262176 | tf_op jit(solution)/shard_map/all_to_all | solution.py:120
  72.0 187.1 %while.21 = (s32[]{:T(128)}, f32[128,512]{1,0:T(8,128)}, f32[9,8,128]{2,1,0:T(8,128)}, f32[8,128,128]{2,0,1:T(8,128)}, s32[4]{0:T(128)S(1)}, /*index=5*/s32[4]{0...) while((s32[]{:T(128)}, f32[128,512]{1,0:T(8,128)}, ...), condition=%wide.region_13.14_spmd.clone.clone, body=%wide.region_0.13_spmd.clone.clone.sunk | while | flops 448201472 | bytes 62394652 | solution.py:110
  87.6 2.2 exponential_multiply_fusion.2
  95.4 1.8 fusion.171
  105.3 3.4 fusion.167
  113.0 2.3 fusion.168
  133.6 2.2 exponential_multiply_fusion.2
  141.4 1.8 fusion.171
  145.9 2.3 convolution_add_fusion.8
  152.3 3.4 fusion.167
  160.0 2.3 fusion.168
  180.6 2.2 exponential_multiply_fusion.2
  188.4 1.8 fusion.171
  193.0 2.3 convolution_add_fusion.8
  199.4 3.4 fusion.167
  207.1 2.3 fusion.168
  227.6 2.2 exponential_multiply_fusion.2
  235.4 1.8 fusion.171
  240.0 2.3 convolution_add_fusion.8
  246.4 3.4 fusion.167
  254.1 2.3 fusion.168
  260.2 26.0 %all_to_all.36 = f32[128,8,128]{2,1,0:T(8,128)S(1)} all-to-all(f32[128,8,128]{2,1,0:T(8,128)S(1)} %bitcast.322), channel_id=1, replica_groups=mesh['gs'=128,'view'=4] {'gs'}, dimensions={0} | all-to-all | bytes 1048576 | tf_op jit(solution)/shard_map/all_to_all | solution.py:132
  286.2 4.0 scatter_custom_fusion
  292.0 8.2 %all-to-all-start.3 = ((f32[9,128,8]{0,2,1:T(8,128)}), f32[9,128,8]{0,2,1:T(8,128)S(1)}, u32[]{:S(2)}, u32[]{:S(2)}) async-start(f32[9,128,8]{0,2,1:T(8,128)} %bitcast.13), calls=%async_computation.3 | async-start | bytes 1048576 | tf_op jit(solution)/shard_map/all_to_all | solution.py:131
  300.3 39.8 %all-reduce.15.cloned.1.call-done = (f32[1024,128]{1,0:T(8,128)}, f32[128,512]{1,0:T(8,128)}) async-done(((f32[1024,128]{1,0:T(8,128)}, f32[128,512]{1,0:T(8,128)}), (f32[1024,128]{1,0:T(8,128)}, f32[128,512]{1,0:T(8,128)})) %all-reduce.15.cloned.1.call-update) | async-done | bytes 786448 | tf_op jit(solution)/shard_map/psum | solution.py:136
  340.1 3.4 scatter_custom_fusion.1
  345.9 189.0 %all-reduce.13.cloned.1.call-done = f32[128,512]{1,0:T(8,128)} async-done(((f32[128,512]{1,0:T(8,128)}), f32[128,512]{1,0:T(8,128)}) %all-reduce.13.cloned.1.call-update) | async-done | bytes 262160 | tf_op jit(solution)/shard_map/psum | solution.py:139
  (516 shorter events, 135.9 us)
Async XLA Ops:
  7.2 24.3 %copy-start = (bf16[1024,128]{1,0:T(8,128)(2,1)S(1)}, bf16[1024,128]{1,0:T(8,128)(2,1)}, u32[]{:S(2)}) copy-start(bf16[1024,128]{1,0:T(8,128)(2,1)} %param.10) | copy-start | bytes 786436
  14.1 35.8 %all-to-all-start = ((f32[9,128,8]{0,2,1:T(8,128)}), f32[9,128,8]{0,2,1:T(8,128)S(1)}, u32[]{:S(2)}, u32[]{:S(2)}) async-start(f32[9,128,8]{0,2,1:T(8,128)} %bitcast_select_fusion.1), calls=%async_computation | async-start | bytes 1048576 | tf_op jit(solution)/shard_map/all_to_all | solution.py:118
  49.9 21.4 %all-to-all-start.1 = ((bf16[128,8,128]{2,1,0:T(8,128)(2,1)}), bf16[128,8,128]{2,1,0:T(8,128)(2,1)S(1)}, u32[]{:S(2)}, u32[]{:S(2)}) async-start(bf16[128,8,128]{2,1,0:T(8,128)(2,1)} %bitcast_select_fusion.2), calls=%async_computation.1 | async-start | bytes 524288 | tf_op jit(solution)/shard_map/all_to_all | solution.py:120
  58.2 281.9 %all-reduce.15.cloned.1.call-start = ((), (), s32[]{:S(2)}) async-start(), calls=%async_computation.5 | async-start | bytes 1572864 | tf_op jit(solution)/shard_map/psum | solution.py:136
  72.0 13.7 %copy-start.8 = (bf16[8,128,128]{2,1,0:T(8,128)(2,1)}, bf16[8,128,128]{2,1,0:T(8,128)(2,1)S(1)}, u32[]{:S(2)}) copy-start(bf16[8,128,128]{2,1,0:T(8,128)(2,1)S(1)} %get-tuple-element.845) | copy-start | bytes 786436 | tf_op jit(solution)/shard_map/while
  79.6 22.9 %copy-start.21 = (f32[256]{0:T(256)}, f32[256]{0:T(256)S(1)}, u32[]{:S(2)}) copy-start(f32[256]{0:T(256)S(1)} %get-tuple-element.770) | copy-start | bytes 3076 | tf_op jit(solution)/shard_map/while
  79.6 22.9 %copy-start.23 = (f32[256]{0:T(256)}, f32[256]{0:T(256)S(1)}, u32[]{:S(2)}) copy-start(f32[256]{0:T(256)S(1)} %get-tuple-element.767) | copy-start | bytes 3076 | tf_op jit(solution)/shard_map/while
  80.3 19.6 %copy-start.28 = (s32[8]{0:T(128)}, s32[8]{0:T(128)S(1)}, u32[]{:S(2)}) copy-start(s32[8]{0:T(128)S(1)} %get-tuple-element.787) | copy-start | bytes 100 | tf_op jit(solution)/shard_map/while
  82.5 18.9 %copy-start.5 = (f32[9,8,128]{2,0,1:T(8,128)}, f32[9,8,128]{2,0,1:T(8,128)S(1)}, u32[]{:S(2)}) copy-start(f32[9,8,128]{2,0,1:T(8,128)S(1)} %select_bitcast_fusion.2) | copy-start | bytes 110596 | tf_op jit(solution)/shard_map/while
  83.2 19.4 %copy-start.11 = (f32[1,8,128]{2,0,1:T(1,128)}, f32[1,8,128]{2,0,1:T(1,128)S(1)}, u32[]{:S(2)}) copy-start(f32[1,8,128]{2,0,1:T(1,128)S(1)} %get-tuple-element.771) | copy-start | bytes 12292 | tf_op jit(solution)/shard_map/while
  83.8 18.8 %copy-start.16 = (f32[1024]{0:T(1024)}, f32[1024]{0:T(1024)S(1)}, u32[]{:S(2)}) copy-start(f32[1024]{0:T(1024)S(1)} %bitcast_multiply_fusion.8) | copy-start | bytes 12292 | tf_op jit(solution)/shard_map/while
  117.9 13.7 %copy-start.8 = (bf16[8,128,128]{2,1,0:T(8,128)(2,1)}, bf16[8,128,128]{2,1,0:T(8,128)(2,1)S(1)}, u32[]{:S(2)}) copy-start(bf16[8,128,128]{2,1,0:T(8,128)(2,1)S(1)} %get-tuple-element.845) | copy-start | bytes 786436 | tf_op jit(solution)/shard_map/while
  125.6 24.0 %copy-start.21 = (f32[256]{0:T(256)}, f32[256]{0:T(256)S(1)}, u32[]{:S(2)}) copy-start(f32[256]{0:T(256)S(1)} %get-tuple-element.770) | copy-start | bytes 3076 | tf_op jit(solution)/shard_map/while
  125.6 24.0 %copy-start.23 = (f32[256]{0:T(256)}, f32[256]{0:T(256)S(1)}, u32[]{:S(2)}) copy-start(f32[256]{0:T(256)S(1)} %get-tuple-element.767) | copy-start | bytes 3076 | tf_op jit(solution)/shard_map/while
  126.3 19.6 %copy-start.28 = (s32[8]{0:T(128)}, s32[8]{0:T(128)S(1)}, u32[]{:S(2)}) copy-start(s32[8]{0:T(128)S(1)} %get-tuple-element.787) | copy-start | bytes 100 | tf_op jit(solution)/shard_map/while
  128.5 20.0 %copy-start.5 = (f32[9,8,128]{2,0,1:T(8,128)}, f32[9,8,128]{2,0,1:T(8,128)S(1)}, u32[]{:S(2)}) copy-start(f32[9,8,128]{2,0,1:T(8,128)S(1)} %select_bitcast_fusion.2) | copy-start | bytes 110596 | tf_op jit(solution)/shard_map/while
  129.1 20.5 %copy-start.11 = (f32[1,8,128]{2,0,1:T(1,128)}, f32[1,8,128]{2,0,1:T(1,128)S(1)}, u32[]{:S(2)}) copy-start(f32[1,8,128]{2,0,1:T(1,128)S(1)} %get-tuple-element.771) | copy-start | bytes 12292 | tf_op jit(solution)/shard_map/while
  129.7 19.9 %copy-start.16 = (f32[1024]{0:T(1024)}, f32[1024]{0:T(1024)S(1)}, u32[]{:S(2)}) copy-start(f32[1024]{0:T(1024)S(1)} %bitcast_multiply_fusion.8) | copy-start | bytes 12292 | tf_op jit(solution)/shard_map/while
  172.6 24.0 %copy-start.21 = (f32[256]{0:T(256)}, f32[256]{0:T(256)S(1)}, u32[]{:S(2)}) copy-start(f32[256]{0:T(256)S(1)} %get-tuple-element.770) | copy-start | bytes 3076 | tf_op jit(solution)/shard_map/while
  172.6 24.0 %copy-start.23 = (f32[256]{0:T(256)}, f32[256]{0:T(256)S(1)}, u32[]{:S(2)}) copy-start(f32[256]{0:T(256)S(1)} %get-tuple-element.767) | copy-start | bytes 3076 | tf_op jit(solution)/shard_map/while
  173.3 19.6 %copy-start.28 = (s32[8]{0:T(128)}, s32[8]{0:T(128)S(1)}, u32[]{:S(2)}) copy-start(s32[8]{0:T(128)S(1)} %get-tuple-element.787) | copy-start | bytes 100 | tf_op jit(solution)/shard_map/while
  175.5 20.0 %copy-start.5 = (f32[9,8,128]{2,0,1:T(8,128)}, f32[9,8,128]{2,0,1:T(8,128)S(1)}, u32[]{:S(2)}) copy-start(f32[9,8,128]{2,0,1:T(8,128)S(1)} %select_bitcast_fusion.2) | copy-start | bytes 110596 | tf_op jit(solution)/shard_map/while
  176.1 20.5 %copy-start.11 = (f32[1,8,128]{2,0,1:T(1,128)}, f32[1,8,128]{2,0,1:T(1,128)S(1)}, u32[]{:S(2)}) copy-start(f32[1,8,128]{2,0,1:T(1,128)S(1)} %get-tuple-element.771) | copy-start | bytes 12292 | tf_op jit(solution)/shard_map/while
  176.7 19.9 %copy-start.16 = (f32[1024]{0:T(1024)}, f32[1024]{0:T(1024)S(1)}, u32[]{:S(2)}) copy-start(f32[1024]{0:T(1024)S(1)} %bitcast_multiply_fusion.8) | copy-start | bytes 12292 | tf_op jit(solution)/shard_map/while
  219.6 24.0 %copy-start.21 = (f32[256]{0:T(256)}, f32[256]{0:T(256)S(1)}, u32[]{:S(2)}) copy-start(f32[256]{0:T(256)S(1)} %get-tuple-element.770) | copy-start | bytes 3076 | tf_op jit(solution)/shard_map/while
  219.6 24.0 %copy-start.23 = (f32[256]{0:T(256)}, f32[256]{0:T(256)S(1)}, u32[]{:S(2)}) copy-start(f32[256]{0:T(256)S(1)} %get-tuple-element.767) | copy-start | bytes 3076 | tf_op jit(solution)/shard_map/while
  220.3 19.6 %copy-start.28 = (s32[8]{0:T(128)}, s32[8]{0:T(128)S(1)}, u32[]{:S(2)}) copy-start(s32[8]{0:T(128)S(1)} %get-tuple-element.787) | copy-start | bytes 100 | tf_op jit(solution)/shard_map/while
  222.5 20.0 %copy-start.5 = (f32[9,8,128]{2,0,1:T(8,128)}, f32[9,8,128]{2,0,1:T(8,128)S(1)}, u32[]{:S(2)}) copy-start(f32[9,8,128]{2,0,1:T(8,128)S(1)} %select_bitcast_fusion.2) | copy-start | bytes 110596 | tf_op jit(solution)/shard_map/while
  223.2 20.5 %copy-start.11 = (f32[1,8,128]{2,0,1:T(1,128)}, f32[1,8,128]{2,0,1:T(1,128)S(1)}, u32[]{:S(2)}) copy-start(f32[1,8,128]{2,0,1:T(1,128)S(1)} %get-tuple-element.771) | copy-start | bytes 12292 | tf_op jit(solution)/shard_map/while
  223.8 19.9 %copy-start.16 = (f32[1024]{0:T(1024)}, f32[1024]{0:T(1024)S(1)}, u32[]{:S(2)}) copy-start(f32[1024]{0:T(1024)S(1)} %bitcast_multiply_fusion.8) | copy-start | bytes 12292 | tf_op jit(solution)/shard_map/while
  292.0 48.1 %all-to-all-start.3 = ((f32[9,128,8]{0,2,1:T(8,128)}), f32[9,128,8]{0,2,1:T(8,128)S(1)}, u32[]{:S(2)}, u32[]{:S(2)}) async-start(f32[9,128,8]{0,2,1:T(8,128)} %bitcast.13), calls=%async_computation.3 | async-start | bytes 1048576 | tf_op jit(solution)/shard_map/all_to_all | solution.py:131
  300.3 234.6 %all-reduce.13.cloned.1.call-start = ((), (), s32[]{:S(2)}) async-start(), calls=%async_computation.4 | async-start | bytes 524288 | tf_op jit(solution)/shard_map/psum | solution.py:139
  (104 other events, 168.1 us)
Sparse Core Ops, SparseCore 0:
  290.4 49.6 all-reduce.14
  343.3 191.5 all-reduce.12
